TPU v7x, 256 devices: a whole 4x4x8 slice. The times are simulated.
256 devices in a mesh: circ: 64 (over x_lo, y, z), span: 4 (over x_hi, core).
Axes of the slice: x: 4 (x_hi: 2, x_lo: 2; x = x_hi * 2 + x_lo), y: 4, z: 8, core: 2. Of those that a mesh axis runs over, the one named last changes fastest.
Arguments:
- coefficients: float32 [65, 5, 16, 4096], P(None, None, 'span', 'circ'), may hold values from -3 to 3
- local_step: float32 [16, 2048, 256], P('span', 'circ'), may hold values from 0.1 to 0.4
- jacobian: float32 [3, 5, 5], replicated, may hold values from -2.5 to 2.5
- harmonic_numbers: int32 [32], replicated, may hold values from 1 to 64
- nodal_diameter: int32 [1], replicated, may hold values from 1 to 64
Outputs:
- new_state: float32 [5, 16, 2048, 256], P(None, 'span', 'circ')
All inputs are finite; a program needn't handle non-finite values.
Results may differ from a plain program's by a relative error of at most 0.0001.
Values sent between devices are 32-bit elements; how exact they have to be, the bound alone decides.
No kernel may reach another device: no remote copies, remote signals or barrier semaphores. Data moves between devices by JAX's collectives and lax.ppermute only.
A program may use at most 128 MiB of HBM per device.

v0:
```python
import math
import jax
import jax.numpy as jnp
from jax import lax
from jax.sharding import PartitionSpec as P

VARS = 5
PASS_DEV = 2
PITCH = 16
AXIAL = 256
section_weight = 0.5
dissipation = 0.125


def extended(array, sides, width, wrap):
    for axis, dim in sides:
        count, length = (lax.axis_size(axis), array.shape[dim])
        up = [(i, (i + 1) % count) for i in range(count if wrap else count - 1)]
        down = [(j, i) for i, j in up]
        last = lax.slice_in_dim(array, length - width, length, axis=dim)
        initial = lax.slice_in_dim(array, 0, width, axis=dim)
        before = lax.ppermute(last, axis, up)
        after = lax.ppermute(initial, axis, down)
        array = jnp.concatenate([before, array, after], axis=dim)
    return array


def phase_table(harmonic_numbers, nodal_diameter, passages, cycle_count):
    phase_turn = harmonic_numbers[None, :] * nodal_diameter[0] % cycle_count
    phase_turn = phase_turn * passages[:, None] % cycle_count
    phase_angle = phase_turn.astype(jnp.float32) * jnp.float32(2.0 * math.pi / cycle_count)
    mean_column = jnp.ones((passages.shape[0], 1), jnp.float32)
    return jnp.concatenate([mean_column, jnp.cos(phase_angle), jnp.sin(phase_angle)], axis=1)


def section_update(flow_state, span_pad, pitch_pad, jacobian, local_step):
    axial_pad = jnp.pad(flow_state, ((0, 0), (0, 0), (0, 0), (1, 1)))
    neighbours = [
        (span_pad[:, 2:], span_pad[:, :-2]),
        (pitch_pad[:, :, 2:], pitch_pad[:, :, :-2]),
        (axial_pad[:, :, :, 2:], axial_pad[:, :, :, :-2]),
    ]
    resid = jnp.zeros(flow_state.shape, jnp.float32)
    for direction in range(3):
        plus_side, minus_side = neighbours[direction]
        flux_part = jnp.einsum(
            "vw,wsqa->vsqa",
            jacobian[direction],
            0.5 * (plus_side - minus_side),
            precision=lax.Precision.HIGHEST,
        )
        resid = resid + flux_part - dissipation * (plus_side - 2.0 * flow_state + minus_side)
    return flow_state - section_weight * local_step[None] * resid


def send_rims(flow_state):
    return extended(flow_state, (("circ", 2),), 1, True)


def local(coefficients, local_step, jacobian, harmonic_numbers, nodal_diameter):
    layers = coefficients.shape[2]
    cycle_size = lax.axis_size("circ")
    passages_all = PASS_DEV * cycle_size
    first_pass = lax.axis_index("circ") * PASS_DEV
    extra = 0
    owned = (first_pass - extra // 2 + jnp.arange(PASS_DEV + extra, dtype=jnp.int32)) % passages_all
    phases = phase_table(harmonic_numbers, nodal_diameter, owned, passages_all)
    fields = jnp.einsum(
        "pi,ivsc->pvsc",
        phases,
        lax.all_gather(coefficients, "circ", axis=3, tiled=True),
        precision=lax.Precision.HIGHEST,
    )
    fields = fields.reshape(PASS_DEV + extra, VARS, layers, PITCH, AXIAL)
    flow_state = fields.transpose(1, 2, 0, 3, 4).reshape(VARS, layers, PASS_DEV * PITCH, AXIAL)
    pitch_pad = send_rims(flow_state)
    span_pad = extended(flow_state, (("span", 1),), 1, False)
    return section_update(flow_state, span_pad, pitch_pad, jacobian, local_step)


def solution(mesh):
    in_specs = (P(None, None, "span", "circ"), P("span", "circ", None), P(), P(), P())
    out_specs = P(None, "span", "circ", None)
    return jax.shard_map(local, mesh=mesh, in_specs=in_specs, out_specs=out_specs, check_vma=False)
```

profile of v0, /device:TPU:1, one launch (start us, length us, event | category | flops | bytes accessed | tf_op | source)
XLA Modules:
  0.0 546.3 jit_solution(13596435359046372487)
XLA Ops:
  6.5 0.0 all-gather.2.cloned.1.call-start
  6.5 0.7 all-gather.2.cloned.1.call-update
  7.9 0.7 and_select_fusion.2
  8.6 0.1 fusion.29
  8.7 0.8 fusion.39
  9.5 0.9 broadcast_multiply_fusion
  10.5 465.5 %all-gather.2.cloned.1.call-done = f32[65,5,4,4096]{0,3,2,1:T(8,128)} async-done(((f32[65,5,4,64]{0,3,2,1:T(8,128)}), f32[65,5,4,4096]{0,3,2,1:T(8,128)}) %all-gather.2.cloned.1.call-update) | async-done | bytes 21299216 | tf_op jit(solution)/shard_map/all_gather | solution.py:71
  476.0 38.7 %fusion.21 = f32[2,5,4,4096]{3,0,2,1:T(2,128)S(1)} fusion(f32[65,5,4,4096]{0,3,2,1:T(8,128)} %all-gather.2.cloned.1.call-done, f32[2,32]{1,0:T(2,128)S(1)} %get-tuple-element.13, f32[2,32]{1,0:T(2,128)S(1)} %get-tuple-element.12, f32[65]{0:T(128)S(1)} %pad.13.clone), kind=kOutput, calls=%fused_computation.46 | convolution fusion | flops 127795456 | bytes 21955332 | tf_op jit(solution)/shard_map/pi,ivsc->pvsc/dot_general | solution.py:68
  514.7 0.6 reshape.31
  515.3 0.4 copy.6
  515.8 0.1 collective-permute-start.3
  515.9 5.7 %collective-permute-start.2 = (f32[5,4,1,256]{3,0,2,1:T(8,128)S(1)}, f32[5,4,1,256]{3,0,2,1:T(8,128)S(1)}, u32[]{:S(2)}, u32[]{:S(2)}) collective-permute-start(f32[5,4,1,256]{3,0,2,1:T(8,128)S(1)} %get-tuple-element.8), channel_id=1, source_target_pairs={{4,0},{8,4},{12,8},{16,12},{20,16},{24,20},{28,24},{32,28},{36,32}... | collective-permute-start | bytes 61448 | tf_op jit(solution)/shard_map/ppermute | solution.py:23
  521.5 5.6 %collective-permute-start.1 = (f32[5,1,32,256]{3,0,2,1:T(8,128)S(1)}, f32[5,1,32,256]{3,0,2,1:T(8,128)S(1)}, u32[]{:S(2)}, u32[]{:S(2)}) collective-permute-start(f32[5,1,32,256]{3,0,2,1:T(8,128)S(1)} %get-tuple-element.5), channel_id=1, source_target_pairs={{0,1},{1,2},{2,3},{4,5},{5,6},{6,7},{8,9},{9,10},{10,11},{12,13},{... | collective-permute-start | bytes 491528 | tf_op jit(solution)/shard_map/ppermute | solution.py:22
  527.1 2.1 collective-permute-start
  529.2 1.4 convolution_bitcast_fusion
  530.7 0.0 collective-permute-done.3
  530.7 0.0 collective-permute-done.2
  530.7 1.1 convolution_bitcast_fusion.1
  531.8 0.0 collective-permute-done.1
  531.8 4.5 collective-permute-done
  536.3 2.0 fusion.6
  538.4 1.0 copy.10
  (4 shorter events, 0.1 us)
Async XLA Ops:
  6.5 469.5 %all-gather.2.cloned.1.call-start = ((), (), s32[]{:S(2)}) async-start(), calls=%async_computation | async-start | bytes 42598400 | tf_op jit(solution)/shard_map/all_gather | solution.py:71
  515.8 14.9 %collective-permute-start.3 = (f32[5,4,1,256]{3,0,2,1:T(8,128)S(1)}, f32[5,4,1,256]{3,0,2,1:T(8,128)S(1)}, u32[]{:S(2)}, u32[]{:S(2)}) collective-permute-start(f32[5,4,1,256]{3,0,2,1:T(8,128)S(1)} %get-tuple-element.7), channel_id=1, source_target_pairs={{0,4},{4,8},{8,12},{12,16},{16,20},{20,24},{24,28},{28,32},{32,36}... | collective-permute-start | bytes 61448 | tf_op jit(solution)/shard_map/ppermute | solution.py:22
  515.9 14.8 %collective-permute-start.2 = (f32[5,4,1,256]{3,0,2,1:T(8,128)S(1)}, f32[5,4,1,256]{3,0,2,1:T(8,128)S(1)}, u32[]{:S(2)}, u32[]{:S(2)}) collective-permute-start(f32[5,4,1,256]{3,0,2,1:T(8,128)S(1)} %get-tuple-element.8), channel_id=1, source_target_pairs={{4,0},{8,4},{12,8},{16,12},{20,16},{24,20},{28,24},{32,28},{36,32}... | collective-permute-start | bytes 61448 | tf_op jit(solution)/shard_map/ppermute | solution.py:23
  521.5 10.3 %collective-permute-start.1 = (f32[5,1,32,256]{3,0,2,1:T(8,128)S(1)}, f32[5,1,32,256]{3,0,2,1:T(8,128)S(1)}, u32[]{:S(2)}, u32[]{:S(2)}) collective-permute-start(f32[5,1,32,256]{3,0,2,1:T(8,128)S(1)} %get-tuple-element.5), channel_id=1, source_target_pairs={{0,1},{1,2},{2,3},{4,5},{5,6},{6,7},{8,9},{9,10},{10,11},{12,13},{... | collective-permute-start | bytes 491528 | tf_op jit(solution)/shard_map/ppermute | solution.py:22
  527.1 9.2 %collective-permute-start = (f32[5,1,32,256]{3,0,2,1:T(8,128)S(1)}, f32[5,1,32,256]{3,0,2,1:T(8,128)S(1)}, u32[]{:S(2)}, u32[]{:S(2)}) collective-permute-start(f32[5,1,32,256]{3,0,2,1:T(8,128)S(1)} %get-tuple-element.6), channel_id=1, source_target_pairs={{1,0},{2,1},{3,2},{5,4},{6,5},{7,6},{9,8},{10,9},{11,10},{13,12},{... | collective-permute-start | bytes 491528 | tf_op jit(solution)/shard_map/ppermute | solution.py:23
Sparse Core Ops, SparseCore 0:
  9.1 466.8 all-gather.1
where the time goes:
time: 547 us; the launch traced here: 546 us
  waiting for transfers between devices  471 us (86%)
  matrix products  43.3 us (8%)
  between operations  14.2 us (3%)
  starting transfers between devices  13.4 us (2%)
    all_gather x1, waiting for transfers between devices, local(): lax.all_gather(coefficients, 'circ', axis=3, tiled=True)  466 us
    dot_general x1, matrix products, local(): jnp.einsum('pi,ivsc->pvsc', phases, lax.all_gather(coefficients, 'circ',...  38.7 us
  transfers between devices with their start and end apart: 5, of which 2 were waited for; matrix products, arithmetic and copies ran while one was open for 1% of the time, Pallas kernels for 0%

commit v1 on v0

--- a/solution.py
+++ b/solution.py
@@ -68,7 +68,15 @@
     fields = jnp.einsum(
         "pi,ivsc->pvsc",
         phases,
-        lax.all_gather(coefficients, "circ", axis=3, tiled=True),
+        jnp.concatenate(
+            jax.lax.all_to_all(
+                jnp.stack([coefficients for _ in range(jax.lax.axis_size("circ"))], axis=0),
+                "circ",
+                split_axis=0,
+                concat_axis=0,
+            ),
+            axis=3,
+        ),
         precision=lax.Precision.HIGHEST,
     )
     fields = fields.reshape(PASS_DEV + extra, VARS, layers, PITCH, AXIAL)

time: 547 us -> 1240 us (2.27)
  the two profiles are of different devices: /device:TPU:1 before, /device:TPU:60 now
where the time goes in v1:
time: 1240 us
  waiting for transfers between devices  1060 us (85%)
  local copies, waits for them, and re-layouts  123 us (10%)
  matrix products  33.8 us (3%)
  starting transfers between devices  19 us (2%)
    all_to_all x1, waiting for transfers between devices, local(): jax.lax.all_to_all(jnp.stack([coefficients for _ in range(jax.lax.axis_si...  1060 us
    reshape x2, local copies, waits for them, and re-layouts, local(): jnp.concatenate(jax.lax.all_to_all(jnp.stack([coefficients for _ in range...  81.5 us
    dot_general x1, matrix products, local(): jnp.einsum('pi,ivsc->pvsc', phases, jnp.concatenate(jax.lax.all_to_all(jn...  29.2 us
    dot_general x1, local copies, waits for them, and re-layouts, local(): jnp.einsum('pi,ivsc->pvsc', phases, jnp.concatenate(jax.lax.all_to_all(jn...  25.7 us
  transfers between devices with their start and end apart: 5, of which 3 were waited for; matrix products, arithmetic and copies ran while one was open for 0% of the time, Pallas kernels for 0%

profile of v1, /device:TPU:60, one launch (start us, length us, event | category | flops | bytes accessed | tf_op | source)
XLA Modules:
  0.0 1241.5 jit_solution(4097348490797647856)
XLA Ops:
  0.0 14.8 %stack.2 = f32[64,65,5,4,64]{1,4,3,2,0:T(8,128)} broadcast(f32[65,5,4,64]{0,3,2,1:T(8,128)} %param.5), dimensions={1,2,3,4} | broadcast | bytes 21632000 | tf_op jit(solution)/shard_map/stack | solution.py:73
  14.8 0.0 copy-start.2
  14.8 0.0 copy-start.1
  14.8 0.0 copy-start
  14.8 12.4 all-to-all-start
  27.9 0.0 copy-done.2
  27.9 0.1 fusion.33
  28.0 0.0 copy-done.1
  28.0 0.0 copy-done
  28.1 1058.6 %all-to-all-done = f32[64,65,5,4,64]{1,4,3,2,0:T(8,128)} async-done(((f32[64,65,5,4,64]{1,4,3,2,0:T(8,128)}), f32[64,65,5,4,64]{1,4,3,2,0:T(8,128)}, u32[]{:S(2)}, u32[]{:S(2)}) %all-to-all-start) | async-done | bytes 21299232 | tf_op jit(solution)/shard_map/all_to_all | solution.py:72
  1086.7 45.6 %copy.30 = f32[65,5,4,64,64]{4,3,2,1,0:T(8,128)} copy(f32[65,5,4,64,64]{0,4,2,1,3:T(8,128)} %bitcast.3) | data formatting | bytes 42598400 | tf_op jit(solution)/shard_map/reshape | solution.py:71
  1132.3 35.9 %reshape.39 = f32[65,5,4,4096]{3,2,1,0:T(4,128)} reshape(f32[65,5,4,64,64]{4,3,2,1,0:T(8,128)} %copy.30) | data formatting | bytes 42598400 | tf_op jit(solution)/shard_map/reshape | solution.py:71
  1168.2 25.7 %reshape.45 = f32[5,4,16,256,65]{3,2,1,0,4:T(8,128)} reshape(f32[5,4,4096,65]{2,1,0,3:T(4,128)} %bitcast.69) | data formatting | bytes 42598400 | tf_op jit(solution)/shard_map/pi,ivsc->pvsc/dot_general | solution.py:68
  1193.9 29.2 %fusion.9 = f32[5,4,2,16,256]{4,2,3,1,0:T(2,128)S(1)} fusion(f32[5,4,16,256,65]{3,2,1,0,4:T(8,128)} %reshape.45, f32[2,32]{1,0:T(2,128)S(1)} %get-tuple-element.13, f32[2,32]{1,0:T(2,128)S(1)} %get-tuple-element.12, f32[65]{0:T(128)S(1)} %pad.13.clone), kind=kOutput, calls=%fused_computation.14 | convolution fusion | flops 127795456 | bytes 21955332 | tf_op jit(solution)/shard_map/pi,ivsc->pvsc/dot_general | solution.py:68
  1223.1 0.4 copy.55
  1223.6 1.4 convolution_bitcast_fusion
  1225.0 0.3 collective-permute-start.2
  1225.3 2.0 collective-permute-start.3
  1227.3 1.9 collective-permute-start
  1229.2 2.4 collective-permute-start.1
  1231.7 0.0 collective-permute-done.2
  1231.7 0.0 collective-permute-done.3
  1231.7 1.1 convolution_bitcast_fusion.1
  1232.8 0.3 collective-permute-done
  1233.1 5.3 collective-permute-done.1
  1238.4 2.0 fusion.8
  1240.5 1.0 copy.48
  (7 shorter events, 0.1 us)
Async XLA Ops:
  14.8 13.1 %copy-start.2 = (s32[32]{0:T(128)S(1)}, s32[32]{0:T(128)}, u32[]{:S(2)}) copy-start(s32[32]{0:T(128)} %param.8) | copy-start | bytes 388
  14.8 13.3 %copy-start.1 = (f32[3,5,5]{2,0,1:T(4,128)S(1)}, f32[3,5,5]{2,0,1:T(4,128)}, u32[]{:S(2)}) copy-start(f32[3,5,5]{2,0,1:T(4,128)} %param.7) | copy-start | bytes 904
  14.8 13.3 %copy-start = (f32[4,32,256]{2,1,0:T(8,128)S(1)}, f32[4,32,256]{2,1,0:T(8,128)}, u32[]{:S(2)}) copy-start(f32[4,32,256]{2,1,0:T(8,128)} %param.6) | copy-start | bytes 393220
  14.8 1071.9 %all-to-all-start = ((f32[64,65,5,4,64]{1,4,3,2,0:T(8,128)}), f32[64,65,5,4,64]{1,4,3,2,0:T(8,128)}, u32[]{:S(2)}, u32[]{:S(2)}) async-start(f32[64,65,5,4,64]{1,4,3,2,0:T(8,128)} %stack.2), calls=%async_computation | async-start | bytes 83886080 | tf_op jit(solution)/shard_map/all_to_all | solution.py:72
  1225.0 6.7 collective-permute-start.2
  1225.3 6.4 collective-permute-start.3
  1227.3 5.8 collective-permute-start
  1229.2 9.2 collective-permute-start.1
